TPU v7x, 512 devices: a whole 4x4x16 slice. The times are simulated.
512 devices in a mesh: group: 16 (over x, z_hi), shard: 32 (over z_lo, y, core).
Axes of the slice: x: 4, y: 4, z: 16 (z_hi: 4, z_lo: 4; z = z_hi * 4 + z_lo), core: 2. Of those that a mesh axis runs over, the one named last changes fastest.
Arguments:
- step_count: int32 [1], replicated, may hold values from 2 to 8
- block_order: int32 [224], replicated, may hold values from 0 to 223, as said below
- saved_tiles: bfloat16 [512, 4, 18, 18, 256], P(('group', 'shard')), may hold values from -6 to 6
- pre_act: bfloat16 [262144, 256], P(('group', 'shard')), may hold values from -6 to 6
- grad_output: bfloat16 [262144, 256], P(('group', 'shard')), may hold values from -0.0234375 to 0.0234375
- pointwise_live: bfloat16 [256, 256], replicated, may hold values from -0.375 to 0.375
- master_rows: float32 [7168, 256], P('shard'), may hold values from -0.25 to 0.25, as said below
- row_moment: float32 [7168], P('shard'), may hold values from 0.5 to 30, as said below
- col_moment: float32 [2, 256], replicated, may hold values from 0.03 to 0.3
- next_tiles: bfloat16 [512, 4, 18, 18, 256], P(('group', 'shard')), may hold values from -6 to 6
Outputs:
- update_rows: float32 [7168, 256], P('shard')
- new_master: float32 [7168, 256], P('shard')
- new_row_moment: float32 [7168], P('shard')
- new_col_moment: float32 [2, 256], replicated
- next_output: bfloat16 [262144, 256], P(('group', 'shard'))
Inputs may be any that keep to these rules, and one draw needn't show every extreme that they name: `block_order`: a permutation of 0 to 223. `master_rows`: rows of the 3x3x3 kernel are of order (6912) ** -0.5 and rows of the 1x1x1 kernel of order 256 ** -0.5. `row_moment`: positive row factors.
All inputs are finite; a program needn't handle non-finite values.
Results may differ from a plain program's by a relative error of at most 0.023.
Values may be sent and summed in bfloat16 or wider, within the bound.
A program may use at most 64 MiB of HBM per device.

v0:
```python
import jax
import jax.numpy as jnp
from jax import lax
from jax.sharding import PartitionSpec as P

CI = 256
CO = 256
BLK = 32
FR = 2
HW = 16
NB3 = 216
NB = 224
learn_rate = 0.002
decay_power = 0.8


def silu_slope(values):
    sigma = jax.nn.sigmoid(values)
    return sigma * (1.0 + values * (1.0 - sigma))


def tap_views(frames):
    views = []
    for frame_off in range(3):
        for row_off in range(3):
            for col_off in range(3):
                window = frames[
                    frame_off : frame_off + FR, row_off : row_off + HW, col_off : col_off + HW, :
                ]
                views.append(window.reshape(FR * HW * HW, CI))
    return views


def contract_rows(left, right):
    return lax.dot_general(
        left, right, (((0,), (0,)), ((), ())), preferred_element_type=jnp.float32
    )


def kernel_sums(values, is_small):
    large_part = jnp.sum(jnp.where(is_small[:, None], 0.0, values), axis=0)
    small_part = jnp.sum(jnp.where(is_small[:, None], values, 0.0), axis=0)
    return jnp.stack([large_part, small_part])


def shards(
    step_count,
    block_order,
    saved_tiles,
    pre_act,
    grad_output,
    pointwise_live,
    master_rows,
    row_moment,
    col_moment,
    next_tiles,
):
    pre_float = pre_act.astype(jnp.float32)
    activation = jax.nn.silu(pre_float).astype(jnp.bfloat16)
    grad_act = lax.dot_general(
        grad_output, pointwise_live, (((1,), (1,)), ((), ())), preferred_element_type=jnp.float32
    )
    grad_pre = (grad_act * silu_slope(pre_float)).astype(jnp.bfloat16)
    pieces = [contract_rows(view, grad_pre) for view in tap_views(saved_tiles[0])]
    pieces.append(contract_rows(activation, grad_output))
    own_term = jnp.concatenate(pieces, axis=0).astype(jnp.bfloat16)
    total_rows = NB * BLK
    stored = jnp.take(own_term.reshape(NB, BLK, CO), block_order, axis=0).reshape(total_rows, CO)
    own_rows = master_rows.shape[0]
    partial_value = lax.psum_scatter(stored, "shard", scatter_dimension=0, tiled=True).astype(
        jnp.float32
    )
    gradient = lax.psum(partial_value, "group")
    owner = lax.axis_index("shard")
    own_count = own_rows // BLK
    own_blocks = lax.dynamic_slice_in_dim(block_order, owner * own_count, own_count)
    is_small = jnp.repeat(own_blocks >= NB3, BLK, total_repeat_length=own_rows)
    decay_rate = 1.0 - step_count.astype(jnp.float32)[0] ** (-decay_power)
    counts = jnp.array([27 * CI, CO], jnp.float32)
    squares = gradient * gradient
    new_row = decay_rate * row_moment + (1.0 - decay_rate) * jnp.mean(squares, axis=1)
    col_part = kernel_sums(squares, is_small)
    row_part = kernel_sums(new_row[:, None], is_small)[:, 0]
    col_total, row_total = lax.psum((col_part, row_part), "shard")
    new_col = decay_rate * col_moment + (1.0 - decay_rate) * col_total / counts[:, None]
    row_mean = row_total / counts
    col_rows = jnp.where(is_small[:, None], new_col[1], new_col[0])
    mean_rows = jnp.where(is_small, row_mean[1], row_mean[0])
    scaled = gradient / jnp.sqrt(new_row[:, None] * col_rows / mean_rows[:, None])
    square_part = kernel_sums(jnp.sum(scaled * scaled, axis=1)[:, None], is_small)[:, 0]
    square_total = lax.psum(square_part, "shard")
    clip_factor = jnp.maximum(1.0, jnp.sqrt(square_total / (counts * CO)))
    update_rows = scaled / jnp.where(is_small, clip_factor[1], clip_factor[0])[:, None]
    new_master = master_rows - learn_rate * update_rows
    weights_low = new_master.astype(jnp.bfloat16)
    gathered = lax.all_gather(weights_low, "shard", axis=0, tiled=True)
    inverse = jnp.zeros((NB,), jnp.int32).at[block_order].set(jnp.arange(NB, dtype=jnp.int32))
    natural = jnp.take(gathered.reshape(NB, BLK, CO), inverse, axis=0).reshape(total_rows, CO)
    spatial = natural[: 27 * CI].reshape(27, CI, CO)
    pointwise = natural[27 * CI :]
    hidden_sum = jnp.zeros((FR * HW * HW, CO), jnp.float32)
    for index_tap, view in enumerate(tap_views(next_tiles[0])):
        hidden_sum = hidden_sum + jnp.dot(
            view, spatial[index_tap], preferred_element_type=jnp.float32
        )
    hidden_act = jax.nn.silu(hidden_sum).astype(jnp.bfloat16)
    next_output = jnp.dot(hidden_act, pointwise, preferred_element_type=jnp.float32).astype(
        jnp.bfloat16
    )
    return (update_rows, new_master, new_row, new_col, next_output)


def solution(mesh):
    in_specs = (
        P(),
        P(),
        P(("group", "shard"), None, None, None, None),
        P(("group", "shard"), None),
        P(("group", "shard"), None),
        P(),
        P("shard", None),
        P("shard"),
        P(),
        P(("group", "shard"), None, None, None, None),
    )
    out_specs = (P("shard", None), P("shard", None), P("shard"), P(), P(("group", "shard"), None))
    return jax.shard_map(shards, mesh=mesh, in_specs=in_specs, out_specs=out_specs, check_vma=False)
```

profile of v0, /device:TPU:1, one launch (start us, length us, event | category | flops | bytes accessed | tf_op | source)
XLA Modules:
  0.0 556.7 jit_solution(18183779678937260853)
XLA Ops:
  7.2 1.3 copy.102
  16.6 0.9 fusion.28
  23.1 0.9 fusion.42
  25.9 0.9 fusion.48
  27.8 0.9 fusion.52
  32.5 0.9 fusion.62
  35.3 1.0 fusion.12
  36.3 4.9 gather_fusion
  41.2 3.8 broadcast_select_fusion.1
  46.8 4.5 select_select_fusion
  51.3 150.8 %reduce-scatter.2.cloned.1.call-done = bf16[224,256]{1,0:T(8,128)(2,1)} async-done(((bf16[7168,256]{1,0:T(8,128)(2,1)}), bf16[224,256]{1,0:T(8,128)(2,1)}) %reduce-scatter.2.cloned.1.call-update) | async-done | bytes 114704 | tf_op jit(solution)/shard_map/reduce_scatter | solution.py:70
  202.1 89.2 %all-reduce.2 = f32[224,256]{1,0:T(8,128)S(1)} all-reduce(bf16[224,256]{1,0:T(8,128)(2,1)} %reduce-scatter.2.cloned.1.call-done), channel_id=1, replica_groups=mesh['group'=16,'shard'=32] {'group'}, use_global_device_ids=true, to_apply=%region_1.3 | all-reduce | flops 57344 | bytes 344064 | tf_op jit(solution)/shard_map/psum | solution.py:73
  291.5 5.2 select_reduce_fusion.5
  296.7 1.3 maximum_bitcast_fusion
  298.0 84.7 %all-reduce = (f32[2]{0:T(128)S(1)}, f32[2,256]{1,0:T(2,128)S(1)}) all-reduce(f32[2]{0:T(128)S(1)} %maximum_bitcast_fusion, f32[2,256]{1,0:T(2,128)S(1)} %pad_maximum_fusion), channel_id=1, replica_groups=mesh['group'=16,'shard'=32] {'shard'}, use_global_device_ids=true, to_apply=%region_8.10 | all-reduce | flops 514 | bytes 4112 | tf_op jit(solution)/shard_map/psum | solution.py:84
  383.3 5.7 %broadcast_select_fusion.3 = f32[224]{0:T(256)S(1)} fusion(f32[]{:T(128)} %bitcast.74, f32[]{:T(128)} %bitcast.73, pred[]{:T(512)} %bitcast.65, pred[]{:T(512)} %bitcast.64, pred[]{:T(512)} %bitcast.63, pred[]{:T(512)} %bitcast.62, pred[]{:T(512)} %bitcast.61, pred[]{:T(512)} %bitcast.60, pred[]{:T(512)} %bitcast.59, s32[256]{0:T(256)S(1)} %add_bitcast_fusion), kind=kLoop, calls=%fused_computation.172 | loop fusion | flops 4704 | bytes 1807 | tf_op jit(solution)/shard_map/jit(_where)/select_n | solution.py:88
  389.3 5.2 select_reduce_fusion.3
  394.5 1.3 maximum_bitcast_fusion.1
  395.8 67.4 %psum.31 = f32[2]{0:T(128)S(1)} all-reduce(f32[2]{0:T(128)S(1)} %maximum_bitcast_fusion.1), channel_id=1, replica_groups=mesh['group'=16,'shard'=32] {'shard'}, use_global_device_ids=true, to_apply=%region_12.14 | all-reduce | flops 2 | bytes 16 | tf_op jit(solution)/shard_map/psum | solution.py:91
  463.8 5.7 %broadcast_select_fusion.2 = f32[224]{0:T(256)S(1)} fusion(f32[]{:T(128)} %bitcast.79, f32[]{:T(128)} %bitcast.78, pred[]{:T(512)} %bitcast.65, pred[]{:T(512)} %bitcast.64, pred[]{:T(512)} %bitcast.63, pred[]{:T(512)} %bitcast.62, pred[]{:T(512)} %bitcast.61, pred[]{:T(512)} %bitcast.60, pred[]{:T(512)} %bitcast.59, s32[256]{0:T(256)S(1)} %add_bitcast_fusion), kind=kLoop, calls=%fused_computation.171 | loop fusion | flops 4704 | bytes 1807 | tf_op jit(solution)/shard_map/jit(_where)/select_n | solution.py:93
  470.5 1.5 scatter_custom_fusion
  472.1 1.4 fusion.85
  473.5 2.1 fusion.84
  475.6 53.3 %all-gather.2.cloned.1.call-done = bf16[7168,256]{1,0:T(8,128)(2,1)} async-done(((bf16[224,256]{1,0:T(8,128)(2,1)}), bf16[7168,256]{1,0:T(8,128)(2,1)}) %all-gather.2.cloned.1.call-update) | async-done | bytes 3670032 | tf_op jit(solution)/shard_map/all_gather | solution.py:96
  528.9 4.9 gather_fusion.1
  533.8 2.5 broadcast_select_fusion
  536.4 1.0 fusion.82
  539.0 1.0 convolution_bitcast_fusion.6
  540.1 1.0 convolution_bitcast_fusion.7
  541.1 1.1 convolution_bitcast_fusion.8
  545.9 1.1 fusion.10
  547.0 2.9 convolution_convert_fusion
  (140 shorter events, 30.9 us)
Async XLA Ops:
  7.2 2.3 copy-start
  7.2 194.9 %reduce-scatter.2.cloned.1.call-start = ((), (), s32[]{:S(2)}) async-start(), calls=%async_computation.1 | async-start | bytes 3784704 | tf_op jit(solution)/shard_map/reduce_scatter | solution.py:70
  45.0 1.8 copy-start.28
  45.0 246.5 %copy-start.26 = (f32[224]{0:T(256)S(1)}, f32[224]{0:T(256)}, u32[]{:S(2)}) copy-start(f32[224]{0:T(256)} %param.22) | copy-start | bytes 2692
  45.0 337.7 %copy-start.25 = (f32[2,256]{1,0:T(2,128)S(1)}, f32[2,256]{1,0:T(2,128)}, u32[]{:S(2)}) copy-start(f32[2,256]{1,0:T(2,128)} %param.23) | copy-start | bytes 6148
  45.0 337.7 %copy-start.29 = (f32[2]{0:T(128)S(1)}, f32[2]{0:T(128)}, u32[]{:S(2)}) copy-start(f32[2]{0:T(128)} %constant.126) | copy-start | bytes 28
  45.0 418.2 %copy-start.32 = (f32[2]{0:T(128)S(1)}, f32[2]{0:T(128)}, u32[]{:S(2)}) copy-start(f32[2]{0:T(128)} %constant.129) | copy-start | bytes 28
  45.0 424.5 %copy-start.22 = (f32[224,256]{1,0:T(8,128)S(1)}, f32[224,256]{1,0:T(8,128)}, u32[]{:S(2)}) copy-start(f32[224,256]{1,0:T(8,128)} %param.21) | copy-start | bytes 688132
  45.0 426.9 %copy-start.21 = (bf16[1,4,18,18,256]{4,1,3,2,0:T(4,128)(2,1)S(1)}, bf16[1,4,18,18,256]{4,1,3,2,0:T(4,128)(2,1)}, u32[]{:S(2)}) copy-start(bf16[1,4,18,18,256]{4,1,3,2,0:T(4,128)(2,1)} %param.24) | copy-start | bytes 1990660
  45.0 483.9 %all-gather.2.cloned.1.call-start = ((), (), s32[]{:S(2)}) async-start(), calls=%async_computation.2 | async-start | bytes 3784704 | tf_op jit(solution)/shard_map/all_gather | solution.py:96
  296.7 176.9 %copy-start.24 = (f32[224]{0:T(256)}, f32[224]{0:T(256)S(1)}, u32[]{:S(2)}) copy-start(f32[224]{0:T(256)S(1)} %get-tuple-element.32) | copy-start | bytes 2692
  382.7 90.8 %copy-start.23 = (f32[2,256]{1,0:T(2,128)}, f32[2,256]{1,0:T(2,128)S(1)}, u32[]{:S(2)}) copy-start(f32[2,256]{1,0:T(2,128)S(1)} %multiply_add_fusion) | copy-start | bytes 6148
  537.4 1.4 copy-start.4
  537.4 1.7 copy-start.3
  537.4 2.7 copy-start.2
  537.6 3.5 copy-start.1
  537.8 4.3 copy-start.20
  538.3 4.1 copy-start.19
  538.5 4.1 copy-start.18
  539.0 3.9 copy-start.17
  540.1 3.1 copy-start.16
  542.2 1.3 copy-start.14
  542.4 1.3 copy-start.12
  542.6 1.3 copy-start.15
  542.9 1.3 copy-start.13
  543.2 1.3 copy-start.11
  543.4 1.3 copy-start.10
  543.7 1.3 copy-start.9
  543.9 1.3 copy-start.8
  544.2 1.2 copy-start.7
  544.4 1.2 copy-start.6
  544.7 1.2 copy-start.5
  (3 other events, 2.6 us)
Sparse Core Ops, SparseCore 0:
  45.2 156.8 reduce-scatter.1
  470.6 58.3 all-gather.1
where the time goes:
time: 557 us
  blocking collectives  241 us (43%)
  waiting for transfers between devices  204 us (37%)
  matrix products  38.5 us (7%)
  other arithmetic  36.8 us (7%)
  local copies, waits for them, and re-layouts  20.3 us (4%)
  between operations  15.6 us (3%)
    reduce_scatter x1, waiting for transfers between devices, shards(): lax.psum_scatter(stored, 'shard', scatter_dimension=0, tiled=True)  151 us
    psum x1, blocking collectives, shards(): gradient = lax.psum(partial_value, 'group')  89.2 us
    psum x1, blocking collectives, shards(): col_total, row_total = lax.psum((col_part, row_part), 'shard')  84.7 us
    psum x1, blocking collectives, shards(): square_total = lax.psum(square_part, 'shard')  67.4 us
    all_gather x1, waiting for transfers between devices, shards(): gathered = lax.all_gather(weights_low, 'shard', axis=0, tiled=True)  53.3 us
    dot_general x28, matrix products, contract_rows(): lax.dot_general(left, right, (((0,), (0,)), ((), ())), preferred_element_...  26.2 us
  transfers between devices with their start and end apart: 2, of which 2 were waited for; matrix products, arithmetic and copies ran while one was open for 2% of the time, Pallas kernels for 0%

commit v1 on v0

--- a/solution.py
+++ b/solution.py
@@ -70,7 +70,7 @@
     partial_value = lax.psum_scatter(stored, "shard", scatter_dimension=0, tiled=True).astype(
         jnp.float32
     )
-    gradient = lax.psum(partial_value, "group")
+    gradient = jnp.sum(lax.all_gather(partial_value, "group"), axis=0)
     owner = lax.axis_index("shard")
     own_count = own_rows // BLK
     own_blocks = lax.dynamic_slice_in_dim(block_order, owner * own_count, own_count)

time: 557 us -> 585 us (1.050)
  waiting for transfers between devices: 204 us -> 332 us
  blocking collectives: 241 us -> 138 us
    all_gather x0 -> x1, waiting for transfers between devices: none -> 119 us  [shards(): gradient = jnp.sum(lax.all_gather(partial_value, 'group'), axis=0)]
    psum x1 -> x0, blocking collectives: 89.2 us -> none  [shards(): gradient = lax.psum(partial_value, 'group')]
    psum x1, blocking collectives: 84.7 us -> 67.8 us  [shards(): col_total, row_total = lax.psum((col_part, row_part), 'shard')]
    reduce_scatter x1, waiting for transfers between devices: 151 us -> 157 us  [shards(): lax.psum_scatter(stored, 'shard', scatter_dimension=0, tiled=True)]
  transfers between devices with their start and end apart: 2 -> 3, of which waited for: 2 -> 3; matrix products, arithmetic and copies ran while one was open for 2% -> 2% of each run, Pallas kernels for 0% -> 0%
where the time goes in v1:
time: 585 us; the launch traced here: 584 us
  waiting for transfers between devices  332 us (57%)
  blocking collectives  138 us (24%)
  other arithmetic  40.3 us (7%)
  matrix products  38.6 us (7%)
  local copies, waits for them, and re-layouts  20.3 us (3%)
  between operations  15.1 us (3%)
    reduce_scatter x1, waiting for transfers between devices, shards(): lax.psum_scatter(stored, 'shard', scatter_dimension=0, tiled=True)  157 us
    all_gather x1, waiting for transfers between devices, shards(): gradient = jnp.sum(lax.all_gather(partial_value, 'group'), axis=0)  119 us
    psum x1, blocking collectives, shards(): square_total = lax.psum(square_part, 'shard')  70 us
    psum x1, blocking collectives, shards(): col_total, row_total = lax.psum((col_part, row_part), 'shard')  67.8 us
    all_gather x1, waiting for transfers between devices, shards(): gathered = lax.all_gather(weights_low, 'shard', axis=0, tiled=True)  56.1 us
    dot_general x28, matrix products, contract_rows(): lax.dot_general(left, right, (((0,), (0,)), ((), ())), preferred_element_...  26.3 us
  transfers between devices with their start and end apart: 3, of which 3 were waited for; matrix products, arithmetic and copies ran while one was open for 2% of the time, Pallas kernels for 0%

profile of v1, /device:TPU:1, one launch (start us, length us, event | category | flops | bytes accessed | tf_op | source)
XLA Modules:
  0.0 584.2 jit_solution(15771389014226687567)
XLA Ops:
  7.2 1.3 copy.102
  11.0 1.0 fusion.16
  21.3 1.0 fusion.38
  29.7 0.9 fusion.56
  35.4 1.0 fusion.12
  36.4 4.9 gather_fusion
  41.2 3.8 broadcast_select_fusion.1
  45.1 156.9 %reduce-scatter.2.cloned.1.call-done = bf16[224,256]{1,0:T(8,128)(2,1)} async-done(((bf16[7168,256]{1,0:T(8,128)(2,1)}), bf16[224,256]{1,0:T(8,128)(2,1)}) %reduce-scatter.2.cloned.1.call-update) | async-done | bytes 114704 | tf_op jit(solution)/shard_map/reduce_scatter | solution.py:70
  202.1 1.6 all_gather.16
  205.3 4.5 select_select_fusion
  209.8 118.9 %all-gather.6.cloned.1.call-done = f32[3584,256]{1,0:T(8,128)} async-done(((f32[224,256]{1,0:T(8,128)}), f32[3584,256]{1,0:T(8,128)}) %all-gather.6.cloned.1.call-update) | async-done | bytes 3670032 | tf_op jit(solution)/shard_map/all_gather | solution.py:73
  328.7 2.3 reduce_sum.81
  331.2 5.1 select_reduce_fusion.5
  336.2 1.3 maximum_bitcast_fusion
  337.5 67.8 %all-reduce = (f32[2]{0:T(128)S(1)}, f32[2,256]{1,0:T(2,128)S(1)}) all-reduce(f32[2]{0:T(128)S(1)} %maximum_bitcast_fusion, f32[2,256]{1,0:T(2,128)S(1)} %pad_maximum_fusion), channel_id=1, replica_groups=mesh['group'=16,'shard'=32] {'shard'}, use_global_device_ids=true, to_apply=%region_8.10 | all-reduce | flops 514 | bytes 4112 | tf_op jit(solution)/shard_map/psum | solution.py:84
  406.0 5.7 broadcast_select_fusion.3
  412.0 5.1 select_reduce_fusion.3
  417.0 1.3 maximum_bitcast_fusion.1
  418.3 70.0 %psum.23 = f32[2]{0:T(128)S(1)} all-reduce(f32[2]{0:T(128)S(1)} %maximum_bitcast_fusion.1), channel_id=1, replica_groups=mesh['group'=16,'shard'=32] {'shard'}, use_global_device_ids=true, to_apply=%region_12.14 | all-reduce | flops 2 | bytes 16 | tf_op jit(solution)/shard_map/psum | solution.py:91
  488.9 5.7 broadcast_select_fusion.2
  495.5 1.5 scatter_custom_fusion
  497.2 1.4 fusion.85
  498.6 2.1 fusion.84
  500.7 56.1 %all-gather.4.cloned.1.call-done = bf16[7168,256]{1,0:T(8,128)(2,1)} async-done(((bf16[224,256]{1,0:T(8,128)(2,1)}), bf16[7168,256]{1,0:T(8,128)(2,1)}) %all-gather.4.cloned.1.call-update) | async-done | bytes 3670032 | tf_op jit(solution)/shard_map/all_gather | solution.py:96
  556.8 4.9 gather_fusion.1
  561.7 2.5 broadcast_select_fusion
  564.3 1.0 fusion.82
  566.9 1.0 convolution_bitcast_fusion.6
  567.9 1.0 convolution_bitcast_fusion.7
  568.9 1.0 convolution_bitcast_fusion.8
  573.7 1.1 fusion.10
  574.8 2.9 convolution_convert_fusion
  (144 shorter events, 32.8 us)
Async XLA Ops:
  7.2 2.3 copy-start
  7.2 194.9 %reduce-scatter.2.cloned.1.call-start = ((), (), s32[]{:S(2)}) async-start(), calls=%async_computation.1 | async-start | bytes 3784704 | tf_op jit(solution)/shard_map/reduce_scatter | solution.py:70
  45.0 160.2 %copy-start.28 = (s32[2,128]{1,0:T(2,128)S(1)}, s32[2,128]{1,0:T(2,128)}, u32[]{:S(2)}) copy-start(s32[2,128]{1,0:T(2,128)} %constant.112.clone.1) | copy-start | bytes 3076
  45.0 286.1 %copy-start.26 = (f32[224]{0:T(256)S(1)}, f32[224]{0:T(256)}, u32[]{:S(2)}) copy-start(f32[224]{0:T(256)} %param.22) | copy-start | bytes 2692
  45.0 360.3 %copy-start.25 = (f32[2,256]{1,0:T(2,128)S(1)}, f32[2,256]{1,0:T(2,128)}, u32[]{:S(2)}) copy-start(f32[2,256]{1,0:T(2,128)} %param.23) | copy-start | bytes 6148
  45.0 360.3 %copy-start.29 = (f32[2]{0:T(128)S(1)}, f32[2]{0:T(128)}, u32[]{:S(2)}) copy-start(f32[2]{0:T(128)} %constant.126) | copy-start | bytes 28
  45.0 443.3 %copy-start.32 = (f32[2]{0:T(128)S(1)}, f32[2]{0:T(128)}, u32[]{:S(2)}) copy-start(f32[2]{0:T(128)} %constant.129) | copy-start | bytes 28
  45.0 449.5 %copy-start.22 = (f32[224,256]{1,0:T(8,128)S(1)}, f32[224,256]{1,0:T(8,128)}, u32[]{:S(2)}) copy-start(f32[224,256]{1,0:T(8,128)} %param.21) | copy-start | bytes 688132
  45.1 452.0 %copy-start.21 = (bf16[1,4,18,18,256]{4,1,3,2,0:T(4,128)(2,1)S(1)}, bf16[1,4,18,18,256]{4,1,3,2,0:T(4,128)(2,1)}, u32[]{:S(2)}) copy-start(bf16[1,4,18,18,256]{4,1,3,2,0:T(4,128)(2,1)} %param.24) | copy-start | bytes 1990660
  45.1 283.6 %all-gather.6.cloned.1.call-start = ((), (), s32[]{:S(2)}) async-start(), calls=%async_computation.3 | async-start | bytes 3899392 | tf_op jit(solution)/shard_map/all_gather | solution.py:73
  203.7 353.1 %all-gather.4.cloned.1.call-start = ((), (), s32[]{:S(2)}) async-start(), calls=%async_computation.2 | async-start | bytes 3784704 | tf_op jit(solution)/shard_map/all_gather | solution.py:96
  336.2 162.4 %copy-start.24 = (f32[224]{0:T(256)}, f32[224]{0:T(256)S(1)}, u32[]{:S(2)}) copy-start(f32[224]{0:T(256)S(1)} %get-tuple-element.32) | copy-start | bytes 2692
  405.4 93.2 %copy-start.23 = (f32[2,256]{1,0:T(2,128)}, f32[2,256]{1,0:T(2,128)S(1)}, u32[]{:S(2)}) copy-start(f32[2,256]{1,0:T(2,128)S(1)} %multiply_add_fusion) | copy-start | bytes 6148
  565.2 1.4 copy-start.4
  565.2 1.6 copy-start.3
  565.2 2.7 copy-start.2
  565.4 3.5 copy-start.1
  565.7 4.3 copy-start.20
  566.1 4.1 copy-start.19
  566.4 4.1 copy-start.18
  566.9 3.9 copy-start.17
  567.9 3.1 copy-start.16
  570.0 1.3 copy-start.14
  570.2 1.3 copy-start.12
  570.5 1.3 copy-start.15
  570.7 1.3 copy-start.13
  571.0 1.3 copy-start.11
  571.2 1.3 copy-start.10
  571.5 1.3 copy-start.9
  571.7 1.3 copy-start.8
  572.0 1.2 copy-start.7
  572.2 1.2 copy-start.6
  (4 other events, 3.9 us)
Sparse Core Ops, SparseCore 0:
  45.2 156.8 reduce-scatter.1
  205.7 122.9 all-gather.5
  495.6 61.0 all-gather.3
